TPU v7x, 32 devices: a whole 2x2x4 slice. The times are simulated.
32 devices in a mesh: scen: 8 (over y, x, core), veh: 4 (over z).
Axes of the slice: x: 2, y: 2, z: 4, core: 2. Of those that a mesh axis runs over, the one named last changes fastest.
Arguments:
- start_plan: bfloat16 [128, 3584, 128], P('scen', 'veh'), may hold values from -6 to 6
- linear_cost: bfloat16 [128, 3584, 128], P('scen', 'veh'), may hold values from -12 to 12
- price: bfloat16 [128, 3584, 128], P('scen', 'veh'), may hold values from -6 to 6
- anchor: bfloat16 [8, 3584, 128], P(None, 'veh'), may hold values from -6 to 6
- hessian: bfloat16 [128, 128, 128], P('scen'), as said below
- usage_coef: bfloat16 [3584, 128], P('veh'), may hold values from -1.5 to 1.5
- crew_limit: float32 [128, 350], P('scen'), may hold values from -48 to 48
- crew_dual: float32 [128, 350], P('scen'), may hold values from 0 to 2
- crew_row: int32 [3584], P('veh'), may hold values from 0 to 349
- bundle_of: int32 [128, 1], replicated, may hold values from 0 to 7
- scen_weight: int32 [128], replicated, may hold values from 1 to 8
Outputs:
- new_plan: bfloat16 [128, 3584, 128], P('scen', 'veh')
- new_price: bfloat16 [128, 3584, 128], P('scen', 'veh')
- bundle_mean: bfloat16 [8, 3584, 128], P('scen', 'veh')
- new_dual: float32 [128, 350], P('scen')
- gap: float32 [], replicated
Inputs may be any that keep to these rules, and one draw needn't show every extreme that they name: `bundle_of`: every bundle holds one scenario or more. `hessian`: symmetric.
All inputs are finite; a program needn't handle non-finite values.
Results may differ from a plain program's by a relative error of at most 0.0013.
The roundings to bfloat16 on the way count: a program that leaves them out, or rounds other values in their place, can miss the bound.
Values sent between devices are 32-bit elements; how exact they have to be, the bound alone decides.
A program may use at most 128 MiB of HBM per device.

v0:
```python
import jax
import jax.numpy as jnp
from jax import lax
from jax.sharding import PartitionSpec as P

ITERS = 12
penalty = 1.0
step_size = 0.02
dual_step = 0.02
highest = lax.Precision.HIGHEST


def shards(
    start_plan,
    linear_cost,
    price,
    anchor,
    hessian,
    usage_coef,
    crew_limit,
    crew_dual,
    crew_row,
    bundle_of,
    scen_weight,
):
    local_scen = start_plan.shape[0]
    bundle_count = anchor.shape[0]
    crew_count = crew_limit.shape[1]
    offset = lax.axis_index("scen") * local_scen
    all_bundles = bundle_of[:, 0]
    my_bundles = lax.dynamic_slice_in_dim(all_bundles, offset, local_scen)
    my_weights = lax.dynamic_slice_in_dim(scen_weight, offset, local_scen).astype(jnp.float32)
    bundle_ids = jnp.arange(bundle_count, dtype=jnp.int32)
    selector = (my_bundles[:, None] == bundle_ids[None, :]).astype(jnp.float32)
    anchored = jnp.einsum(
        "sb,bvi->svi", selector.astype(jnp.bfloat16), anchor, preferred_element_type=jnp.float32
    )
    linear_part = linear_cost.astype(jnp.float32) + price.astype(jnp.float32) - penalty * anchored
    coefficient = usage_coef.astype(jnp.float32)
    crew_map = (crew_row[:, None] == jnp.arange(crew_count, dtype=jnp.int32)[None, :]).astype(
        jnp.float32
    )

    def advance(index, state_pair):
        roster, multiplier = state_pair
        rounded = roster.astype(jnp.bfloat16)
        curvature = jnp.einsum("svi,sij->svj", rounded, hessian, preferred_element_type=jnp.float32)
        consumed = jnp.sum(roster * coefficient[None], axis=2)
        partial_use = jnp.dot(consumed, crew_map, precision=highest)
        usage = lax.psum(partial_use, "veh")
        updated = jnp.maximum(multiplier + dual_step * (usage - crew_limit), 0.0)
        per_vehicle = jnp.dot(multiplier, crew_map.T, precision=highest)
        gradient = (
            curvature + linear_part + penalty * roster + per_vehicle[:, :, None] * coefficient[None]
        )
        return (roster - step_size * gradient, updated)

    roster, multiplier = lax.fori_loop(
        0, ITERS, advance, (start_plan.astype(jnp.float32), crew_dual)
    )
    weighted_pick = selector * my_weights[:, None]
    every_weight = jnp.sum(
        (all_bundles[:, None] == bundle_ids[None, :]).astype(jnp.float32)
        * scen_weight.astype(jnp.float32)[:, None],
        axis=0,
    )
    owned_rows = bundle_count // lax.axis_size("scen")
    own_start = lax.axis_index("scen") * owned_rows
    partial_sums = jnp.einsum("sb,svi->bvi", weighted_pick, roster, precision=highest)
    totals = lax.psum(partial_sums, "scen")
    every_mean = totals / every_weight[:, None, None]
    own_mean = lax.dynamic_slice_in_dim(every_mean, own_start, owned_rows)
    mean_here = jnp.einsum("sb,bvi->svi", selector, every_mean, precision=highest)
    deviation = roster - mean_here
    new_price = (price.astype(jnp.float32) + penalty * deviation).astype(jnp.bfloat16)
    spread = jnp.sum(my_weights * jnp.sum(deviation * deviation, axis=(1, 2)))
    spread_total = lax.psum(spread, ("scen", "veh"))
    entries = start_plan.shape[1] * lax.axis_size("veh") * start_plan.shape[2]
    gap = jnp.sqrt(spread_total / (jnp.sum(scen_weight.astype(jnp.float32)) * entries))
    return (roster.astype(jnp.bfloat16), new_price, own_mean.astype(jnp.bfloat16), multiplier, gap)


def solution(mesh):
    return jax.shard_map(
        shards,
        mesh=mesh,
        in_specs=(
            P("scen", "veh", None),
            P("scen", "veh", None),
            P("scen", "veh", None),
            P(None, "veh", None),
            P("scen", None, None),
            P("veh", None),
            P("scen", None),
            P("scen", None),
            P("veh"),
            P(),
            P(),
        ),
        out_specs=(
            P("scen", "veh", None),
            P("scen", "veh", None),
            P("scen", "veh", None),
            P("scen", None),
            P(),
        ),
        check_vma=False,
    )
```

profile of v0, /device:TPU:0, one launch (start us, length us, event | category | flops | bytes accessed | tf_op | source)
XLA Modules:
  0.0 568.2 jit_solution(2180171724463665782)
XLA Ops:
  8.7 22.6 %fusion.12 = f32[16,896,128]{2,0,1:T(8,128)S(1)} fusion(bf16[16,896,128]{2,1,0:T(8,128)(2,1)} %param.14, bf16[16,896,128]{2,1,0:T(8,128)(2,1)} %param.15, bf16[8,896,128]{2,1,0:T(8,128)(2,1)S(1)} %copy-done, s32[16]{0:T(128)S(1)} %dynamic-slice_bitcast_fusion), kind=kOutput, calls=%fused_computation.15 | convolution fusion | flops 36700544 | bytes 16515136 | tf_op jit(solution)/shard_map/sb,bvi->svi/dot_general | solution.py:35
  31.3 5.2 copy.27
  40.4 364.3 %while.13 = (s32[]{:T(128)}, f32[16,896,128]{2,1,0:T(8,128)}, f32[16,350]{1,0:T(8,128)S(1)}, bf16[16,128,128]{2,1,0:T(8,128)(2,1)S(1)}, f32[16,896,128]{2,1,0:T(...) while((s32[]{:T(128)}, f32[16,896,128]{2,1,0:T(8,128)}, ...), condition=%wide.region_3.0_spmd.clone, body=%wide.region_0.0_spmd.clone.sunk | while | flops 607967616 | bytes 75257976 | solution.py:58
  47.0 5.9 %multiply_subtract_fusion.2 = f32[16,896,128]{2,1,0:T(8,128)} fusion(f32[16,896,128]{2,1,0:T(8,128)S(1)} %copy.53, f32[16,896,128]{2,1,0:T(8,128)S(1)} %copy-done.1, f32[896,128]{1,0:T(8,128)S(1)} %get-tuple-element.185, f32[16,896]{1,0:T(8,128)S(1)} %fusion.47, bf16[16,128,128]{2,1,0:T(8,128)(2,1)S(1)} %get-tuple-element.183), kind=kOutput, calls=%fused_computation.2.clone.1 | convolution fusion | flops 482607104 | bytes 23060480 | tf_op jit(solution)/shard_map/while/body/eval_jaxpr/svi,sij->svj/dot_general | solution.py:47
  53.8 20.8 %psum.25 = f32[16,350]{1,0:T(8,128)S(1)} all-reduce(f32[16,350]{1,0:T(8,128)S(1)} %fusion.48), channel_id=1, replica_groups=mesh['scen'=8,'veh'=4] {'veh'}, use_global_device_ids=true, to_apply=%region_2.0 | all-reduce | flops 5600 | bytes 44800 | tf_op jit(solution)/shard_map/while/body/eval_jaxpr/psum | solution.py:50
  81.1 5.9 %multiply_subtract_fusion.2 = f32[16,896,128]{2,1,0:T(8,128)} fusion(f32[16,896,128]{2,1,0:T(8,128)S(1)} %copy.53, f32[16,896,128]{2,1,0:T(8,128)S(1)} %copy-done.1, f32[896,128]{1,0:T(8,128)S(1)} %get-tuple-element.185, f32[16,896]{1,0:T(8,128)S(1)} %fusion.47, bf16[16,128,128]{2,1,0:T(8,128)(2,1)S(1)} %get-tuple-element.183), kind=kOutput, calls=%fused_computation.2.clone.1 | convolution fusion | flops 482607104 | bytes 23060480 | tf_op jit(solution)/shard_map/while/body/eval_jaxpr/svi,sij->svj/dot_general | solution.py:47
  88.0 15.8 %psum.25 = f32[16,350]{1,0:T(8,128)S(1)} all-reduce(f32[16,350]{1,0:T(8,128)S(1)} %fusion.48), channel_id=1, replica_groups=mesh['scen'=8,'veh'=4] {'veh'}, use_global_device_ids=true, to_apply=%region_2.0 | all-reduce | flops 5600 | bytes 44800 | tf_op jit(solution)/shard_map/while/body/eval_jaxpr/psum | solution.py:50
  110.4 5.9 %multiply_subtract_fusion.2 = f32[16,896,128]{2,1,0:T(8,128)} fusion(f32[16,896,128]{2,1,0:T(8,128)S(1)} %copy.53, f32[16,896,128]{2,1,0:T(8,128)S(1)} %copy-done.1, f32[896,128]{1,0:T(8,128)S(1)} %get-tuple-element.185, f32[16,896]{1,0:T(8,128)S(1)} %fusion.47, bf16[16,128,128]{2,1,0:T(8,128)(2,1)S(1)} %get-tuple-element.183), kind=kOutput, calls=%fused_computation.2.clone.1 | convolution fusion | flops 482607104 | bytes 23060480 | tf_op jit(solution)/shard_map/while/body/eval_jaxpr/svi,sij->svj/dot_general | solution.py:47
  117.2 17.4 %psum.25 = f32[16,350]{1,0:T(8,128)S(1)} all-reduce(f32[16,350]{1,0:T(8,128)S(1)} %fusion.48), channel_id=1, replica_groups=mesh['scen'=8,'veh'=4] {'veh'}, use_global_device_ids=true, to_apply=%region_2.0 | all-reduce | flops 5600 | bytes 44800 | tf_op jit(solution)/shard_map/while/body/eval_jaxpr/psum | solution.py:50
  141.2 5.9 %multiply_subtract_fusion.2 = f32[16,896,128]{2,1,0:T(8,128)} fusion(f32[16,896,128]{2,1,0:T(8,128)S(1)} %copy.53, f32[16,896,128]{2,1,0:T(8,128)S(1)} %copy-done.1, f32[896,128]{1,0:T(8,128)S(1)} %get-tuple-element.185, f32[16,896]{1,0:T(8,128)S(1)} %fusion.47, bf16[16,128,128]{2,1,0:T(8,128)(2,1)S(1)} %get-tuple-element.183), kind=kOutput, calls=%fused_computation.2.clone.1 | convolution fusion | flops 482607104 | bytes 23060480 | tf_op jit(solution)/shard_map/while/body/eval_jaxpr/svi,sij->svj/dot_general | solution.py:47
  148.1 15.8 %psum.25 = f32[16,350]{1,0:T(8,128)S(1)} all-reduce(f32[16,350]{1,0:T(8,128)S(1)} %fusion.48), channel_id=1, replica_groups=mesh['scen'=8,'veh'=4] {'veh'}, use_global_device_ids=true, to_apply=%region_2.0 | all-reduce | flops 5600 | bytes 44800 | tf_op jit(solution)/shard_map/while/body/eval_jaxpr/psum | solution.py:50
  170.5 5.9 %multiply_subtract_fusion.2 = f32[16,896,128]{2,1,0:T(8,128)} fusion(f32[16,896,128]{2,1,0:T(8,128)S(1)} %copy.53, f32[16,896,128]{2,1,0:T(8,128)S(1)} %copy-done.1, f32[896,128]{1,0:T(8,128)S(1)} %get-tuple-element.185, f32[16,896]{1,0:T(8,128)S(1)} %fusion.47, bf16[16,128,128]{2,1,0:T(8,128)(2,1)S(1)} %get-tuple-element.183), kind=kOutput, calls=%fused_computation.2.clone.1 | convolution fusion | flops 482607104 | bytes 23060480 | tf_op jit(solution)/shard_map/while/body/eval_jaxpr/svi,sij->svj/dot_general | solution.py:47
  177.3 17.4 %psum.25 = f32[16,350]{1,0:T(8,128)S(1)} all-reduce(f32[16,350]{1,0:T(8,128)S(1)} %fusion.48), channel_id=1, replica_groups=mesh['scen'=8,'veh'=4] {'veh'}, use_global_device_ids=true, to_apply=%region_2.0 | all-reduce | flops 5600 | bytes 44800 | tf_op jit(solution)/shard_map/while/body/eval_jaxpr/psum | solution.py:50
  201.3 5.9 %multiply_subtract_fusion.2 = f32[16,896,128]{2,1,0:T(8,128)} fusion(f32[16,896,128]{2,1,0:T(8,128)S(1)} %copy.53, f32[16,896,128]{2,1,0:T(8,128)S(1)} %copy-done.1, f32[896,128]{1,0:T(8,128)S(1)} %get-tuple-element.185, f32[16,896]{1,0:T(8,128)S(1)} %fusion.47, bf16[16,128,128]{2,1,0:T(8,128)(2,1)S(1)} %get-tuple-element.183), kind=kOutput, calls=%fused_computation.2.clone.1 | convolution fusion | flops 482607104 | bytes 23060480 | tf_op jit(solution)/shard_map/while/body/eval_jaxpr/svi,sij->svj/dot_general | solution.py:47
  208.2 16.0 %psum.25 = f32[16,350]{1,0:T(8,128)S(1)} all-reduce(f32[16,350]{1,0:T(8,128)S(1)} %fusion.48), channel_id=1, replica_groups=mesh['scen'=8,'veh'=4] {'veh'}, use_global_device_ids=true, to_apply=%region_2.0 | all-reduce | flops 5600 | bytes 44800 | tf_op jit(solution)/shard_map/while/body/eval_jaxpr/psum | solution.py:50
  230.7 5.9 %multiply_subtract_fusion.2 = f32[16,896,128]{2,1,0:T(8,128)} fusion(f32[16,896,128]{2,1,0:T(8,128)S(1)} %copy.53, f32[16,896,128]{2,1,0:T(8,128)S(1)} %copy-done.1, f32[896,128]{1,0:T(8,128)S(1)} %get-tuple-element.185, f32[16,896]{1,0:T(8,128)S(1)} %fusion.47, bf16[16,128,128]{2,1,0:T(8,128)(2,1)S(1)} %get-tuple-element.183), kind=kOutput, calls=%fused_computation.2.clone.1 | convolution fusion | flops 482607104 | bytes 23060480 | tf_op jit(solution)/shard_map/while/body/eval_jaxpr/svi,sij->svj/dot_general | solution.py:47
  237.5 17.3 %psum.25 = f32[16,350]{1,0:T(8,128)S(1)} all-reduce(f32[16,350]{1,0:T(8,128)S(1)} %fusion.48), channel_id=1, replica_groups=mesh['scen'=8,'veh'=4] {'veh'}, use_global_device_ids=true, to_apply=%region_2.0 | all-reduce | flops 5600 | bytes 44800 | tf_op jit(solution)/shard_map/while/body/eval_jaxpr/psum | solution.py:50
  261.4 5.9 %multiply_subtract_fusion.2 = f32[16,896,128]{2,1,0:T(8,128)} fusion(f32[16,896,128]{2,1,0:T(8,128)S(1)} %copy.53, f32[16,896,128]{2,1,0:T(8,128)S(1)} %copy-done.1, f32[896,128]{1,0:T(8,128)S(1)} %get-tuple-element.185, f32[16,896]{1,0:T(8,128)S(1)} %fusion.47, bf16[16,128,128]{2,1,0:T(8,128)(2,1)S(1)} %get-tuple-element.183), kind=kOutput, calls=%fused_computation.2.clone.1 | convolution fusion | flops 482607104 | bytes 23060480 | tf_op jit(solution)/shard_map/while/body/eval_jaxpr/svi,sij->svj/dot_general | solution.py:47
  268.3 16.1 %psum.25 = f32[16,350]{1,0:T(8,128)S(1)} all-reduce(f32[16,350]{1,0:T(8,128)S(1)} %fusion.48), channel_id=1, replica_groups=mesh['scen'=8,'veh'=4] {'veh'}, use_global_device_ids=true, to_apply=%region_2.0 | all-reduce | flops 5600 | bytes 44800 | tf_op jit(solution)/shard_map/while/body/eval_jaxpr/psum | solution.py:50
  291.0 5.9 %multiply_subtract_fusion.2 = f32[16,896,128]{2,1,0:T(8,128)} fusion(f32[16,896,128]{2,1,0:T(8,128)S(1)} %copy.53, f32[16,896,128]{2,1,0:T(8,128)S(1)} %copy-done.1, f32[896,128]{1,0:T(8,128)S(1)} %get-tuple-element.185, f32[16,896]{1,0:T(8,128)S(1)} %fusion.47, bf16[16,128,128]{2,1,0:T(8,128)(2,1)S(1)} %get-tuple-element.183), kind=kOutput, calls=%fused_computation.2.clone.1 | convolution fusion | flops 482607104 | bytes 23060480 | tf_op jit(solution)/shard_map/while/body/eval_jaxpr/svi,sij->svj/dot_general | solution.py:47
  297.8 17.1 %psum.25 = f32[16,350]{1,0:T(8,128)S(1)} all-reduce(f32[16,350]{1,0:T(8,128)S(1)} %fusion.48), channel_id=1, replica_groups=mesh['scen'=8,'veh'=4] {'veh'}, use_global_device_ids=true, to_apply=%region_2.0 | all-reduce | flops 5600 | bytes 44800 | tf_op jit(solution)/shard_map/while/body/eval_jaxpr/psum | solution.py:50
  321.5 5.9 %multiply_subtract_fusion.2 = f32[16,896,128]{2,1,0:T(8,128)} fusion(f32[16,896,128]{2,1,0:T(8,128)S(1)} %copy.53, f32[16,896,128]{2,1,0:T(8,128)S(1)} %copy-done.1, f32[896,128]{1,0:T(8,128)S(1)} %get-tuple-element.185, f32[16,896]{1,0:T(8,128)S(1)} %fusion.47, bf16[16,128,128]{2,1,0:T(8,128)(2,1)S(1)} %get-tuple-element.183), kind=kOutput, calls=%fused_computation.2.clone.1 | convolution fusion | flops 482607104 | bytes 23060480 | tf_op jit(solution)/shard_map/while/body/eval_jaxpr/svi,sij->svj/dot_general | solution.py:47
  328.4 16.2 %psum.25 = f32[16,350]{1,0:T(8,128)S(1)} all-reduce(f32[16,350]{1,0:T(8,128)S(1)} %fusion.48), channel_id=1, replica_groups=mesh['scen'=8,'veh'=4] {'veh'}, use_global_device_ids=true, to_apply=%region_2.0 | all-reduce | flops 5600 | bytes 44800 | tf_op jit(solution)/shard_map/while/body/eval_jaxpr/psum | solution.py:50
  351.1 5.9 %multiply_subtract_fusion.2 = f32[16,896,128]{2,1,0:T(8,128)} fusion(f32[16,896,128]{2,1,0:T(8,128)S(1)} %copy.53, f32[16,896,128]{2,1,0:T(8,128)S(1)} %copy-done.1, f32[896,128]{1,0:T(8,128)S(1)} %get-tuple-element.185, f32[16,896]{1,0:T(8,128)S(1)} %fusion.47, bf16[16,128,128]{2,1,0:T(8,128)(2,1)S(1)} %get-tuple-element.183), kind=kOutput, calls=%fused_computation.2.clone.1 | convolution fusion | flops 482607104 | bytes 23060480 | tf_op jit(solution)/shard_map/while/body/eval_jaxpr/svi,sij->svj/dot_general | solution.py:47
  358.0 17.1 %psum.25 = f32[16,350]{1,0:T(8,128)S(1)} all-reduce(f32[16,350]{1,0:T(8,128)S(1)} %fusion.48), channel_id=1, replica_groups=mesh['scen'=8,'veh'=4] {'veh'}, use_global_device_ids=true, to_apply=%region_2.0 | all-reduce | flops 5600 | bytes 44800 | tf_op jit(solution)/shard_map/while/body/eval_jaxpr/psum | solution.py:50
  381.6 5.9 %multiply_subtract_fusion.2 = f32[16,896,128]{2,1,0:T(8,128)} fusion(f32[16,896,128]{2,1,0:T(8,128)S(1)} %copy.53, f32[16,896,128]{2,1,0:T(8,128)S(1)} %copy-done.1, f32[896,128]{1,0:T(8,128)S(1)} %get-tuple-element.185, f32[16,896]{1,0:T(8,128)S(1)} %fusion.47, bf16[16,128,128]{2,1,0:T(8,128)(2,1)S(1)} %get-tuple-element.183), kind=kOutput, calls=%fused_computation.2.clone.1 | convolution fusion | flops 482607104 | bytes 23060480 | tf_op jit(solution)/shard_map/while/body/eval_jaxpr/svi,sij->svj/dot_general | solution.py:47
  388.5 16.2 %psum.25 = f32[16,350]{1,0:T(8,128)S(1)} all-reduce(f32[16,350]{1,0:T(8,128)S(1)} %fusion.48), channel_id=1, replica_groups=mesh['scen'=8,'veh'=4] {'veh'}, use_global_device_ids=true, to_apply=%region_2.0 | all-reduce | flops 5600 | bytes 44800 | tf_op jit(solution)/shard_map/while/body/eval_jaxpr/psum | solution.py:50
  404.8 14.0 %fusion.14 = f32[8,896,128]{2,0,1:T(8,128)} fusion(f32[16,896,128]{2,1,0:T(8,128)} %get-tuple-element.48, f32[16]{0:T(128)S(1)} %dynamic-slice_convert_fusion.1, s32[16]{0:T(128)S(1)} %dynamic-slice_bitcast_fusion), kind=kOutput, calls=%fused_computation.18 | convolution fusion | flops 176161024 | bytes 11010176 | tf_op jit(solution)/shard_map/sb,svi->bvi/dot_general | solution.py:69
  418.8 5.6 convert_element_type.49
  425.8 67.3 %all-reduce.2.cloned.1.call-done = f32[8,896,128]{2,0,1:T(8,128)} async-done(((f32[8,896,128]{2,0,1:T(8,128)}), f32[8,896,128]{2,0,1:T(8,128)}) %all-reduce.2.cloned.1.call-update) | async-done | bytes 3670032 | tf_op jit(solution)/shard_map/psum | solution.py:70
  496.2 17.2 %multiply_reduce_fusion.1 = (f32[16]{0:T(128)S(1)}, bf16[16,896,128]{2,0,1:T(8,128)(2,1)S(1)}) fusion(bf16[16,896,128]{2,1,0:T(8,128)(2,1)S(1)} %copy-done.3, f32[8,896,128]{2,0,1:T(8,128)S(1)} %broadcast_divide_fusion, s32[16]{0:T(128)S(1)} %dynamic-slice_bitcast_fusion, f32[16,896,128]{2,1,0:T(8,128)} %get-tuple-element.48), kind=kOutput, calls=%fused_computation.17 | convolution fusion | flops 187170928 | bytes 18350208 | tf_op jit(solution)/shard_map/sb,bvi->svi/dot_general | solution.py:73
  516.9 39.5 %psum.22 = f32[]{:T(128)} all-reduce(f32[]{:T(128)} %multiply_reduce_fusion.2), channel_id=1, replica_groups=mesh['scen'=8,'veh'=4] {'scen','veh'}, use_global_device_ids=true, to_apply=%region_8.0 | all-reduce | flops 1 | bytes 8 | tf_op jit(solution)/shard_map/psum | solution.py:77
  (122 shorter events, 106.0 us)
Async XLA Ops:
  7.2 1.5 copy-start
  7.2 485.9 %all-reduce.2.cloned.1.call-start = ((), (), s32[]{:S(2)}) async-start(), calls=%async_computation | async-start | bytes 7340032 | tf_op jit(solution)/shard_map/psum | solution.py:70
  31.3 5.2 copy-start.5
  36.5 3.8 copy-start.9
  36.5 3.8 copy-start.4
  36.5 3.9 copy-start.7
  36.5 3.9 copy-start.8
  36.5 3.9 copy-start.11
  40.4 364.3 %copy-start.10 = (s32[128]{0:T(128)S(1)}, s32[128]{0:T(128)}, u32[]{:S(2)}) copy-start(s32[128]{0:T(128)} %param.23) | copy-start | bytes 1540
  43.5 3.5 copy-start.1
  77.7 3.5 copy-start.1
  106.9 3.5 copy-start.1
  137.8 3.5 copy-start.1
  167.0 3.5 copy-start.1
  197.9 3.5 copy-start.1
  227.2 3.5 copy-start.1
  258.0 3.5 copy-start.1
  287.5 3.5 copy-start.1
  318.1 3.5 copy-start.1
  347.7 3.5 copy-start.1
  378.1 3.5 copy-start.1
  404.7 14.1 %copy-start.6 = (f32[16,350]{1,0:T(8,128)}, f32[16,350]{1,0:T(8,128)S(1)}, u32[]{:S(2)}) copy-start(f32[16,350]{1,0:T(8,128)S(1)} %get-tuple-element.93) | copy-start | bytes 67204
  418.7 6.9 %copy-start.12 = (s32[128,1]{0,1:T(1,128)S(1)}, s32[128,1]{0,1:T(1,128)}, u32[]{:S(2)}) copy-start(s32[128,1]{0,1:T(1,128)} %param.22) | copy-start | bytes 1540
  493.1 3.1 copy-start.3
  496.2 17.2 %copy-start.2 = (f32[8,896,128]{2,0,1:T(8,128)}, f32[8,896,128]{2,0,1:T(8,128)S(1)}, u32[]{:S(2)}) copy-start(f32[8,896,128]{2,0,1:T(8,128)S(1)} %broadcast_divide_fusion) | copy-start | bytes 11010052
Sparse Core Ops, SparseCore 0:
  418.9 74.1 all-reduce.1
where the time goes:
time: 569 us; the launch traced here: 568 us
  blocking collectives  243 us (43%)
  matrix products  152 us (27%)
  waiting for transfers between devices  67.3 us (12%)
  local copies, waits for them, and re-layouts  50.3 us (9%)
  other arithmetic  38.6 us (7%)
  between operations  16.7 us (3%)
    psum x12, blocking collectives, advance(): usage = lax.psum(partial_use, 'veh')  203 us
    dot_general x12, matrix products, advance(): jnp.einsum('svi,sij->svj', rounded, hessian, preferred_element_type=jnp.f...  70.6 us
    psum x1, waiting for transfers between devices, shards(): totals = lax.psum(partial_sums, 'scen')  67.3 us
    psum x1, blocking collectives, shards(): spread_total = lax.psum(spread, ('scen', 'veh'))  39.5 us
    while x36, local copies, waits for them, and re-layouts  37.1 us
    reduce_sum x12, other arithmetic, advance(): consumed = jnp.sum(roster * coefficient[None], axis=2)  25.1 us
    dot_general x1, matrix products, shards(): jnp.einsum('sb,bvi->svi', selector.astype(jnp.bfloat16), anchor, preferre...  22.6 us
    dot_general x1, matrix products, shards(): jnp.einsum('sb,bvi->svi', selector, every_mean, precision=highest)  17.2 us
  transfers between devices with their start and end apart: 1, of which 1 were waited for; matrix products, arithmetic and copies ran while one was open for 1% of the time, Pallas kernels for 0%

commit v1 on v0

--- a/solution.py
+++ b/solution.py
@@ -1,3 +1,4 @@
+import functools
 import jax
 import jax.numpy as jnp
 from jax import lax
@@ -8,6 +9,13 @@
 step_size = 0.02
 dual_step = 0.02
 highest = lax.Precision.HIGHEST
+
+
+def _cut_terms(v0, axis_id):
+    return jnp.sum(lax.all_gather(v0, axis_id), axis=0)
+
+
+shape_zone = functools.partial(_cut_terms, axis_id="veh")
 
 
 def shards(
@@ -47,7 +55,7 @@
         curvature = jnp.einsum("svi,sij->svj", rounded, hessian, preferred_element_type=jnp.float32)
         consumed = jnp.sum(roster * coefficient[None], axis=2)
         partial_use = jnp.dot(consumed, crew_map, precision=highest)
-        usage = lax.psum(partial_use, "veh")
+        usage = shape_zone(partial_use)
         updated = jnp.maximum(multiplier + dual_step * (usage - crew_limit), 0.0)
         per_vehicle = jnp.dot(multiplier, crew_map.T, precision=highest)
         gradient = (

time: 569 us -> 529 us (0.930)
  blocking collectives: 243 us -> 201 us
    psum x12 -> x0, blocking collectives: 203 us -> none  [advance(): usage = lax.psum(partial_use, 'veh')]
    all_gather x0 -> x12, blocking collectives: none -> 162 us  [_cut_terms(): return jnp.sum(lax.all_gather(v0, axis_id), axis=0)]
where the time goes in v1:
time: 529 us
  blocking collectives  201 us (38%)
  matrix products  152 us (29%)
  waiting for transfers between devices  69.1 us (13%)
  local copies, waits for them, and re-layouts  50.3 us (10%)
  other arithmetic  38.7 us (7%)
  between operations  16.7 us (3%)
    all_gather x12, blocking collectives, _cut_terms(): return jnp.sum(lax.all_gather(v0, axis_id), axis=0)  162 us
    dot_general x12, matrix products, advance(): jnp.einsum('svi,sij->svj', rounded, hessian, preferred_element_type=jnp.f...  70.6 us
    psum x1, waiting for transfers between devices, shards(): totals = lax.psum(partial_sums, 'scen')  69 us
    psum x1, blocking collectives, shards(): spread_total = lax.psum(spread, ('scen', 'veh'))  39.5 us
    while x36, local copies, waits for them, and re-layouts  37.1 us
    reduce_sum x12, other arithmetic, advance(): consumed = jnp.sum(roster * coefficient[None], axis=2)  25.1 us
    dot_general x1, matrix products, shards(): jnp.einsum('sb,bvi->svi', selector.astype(jnp.bfloat16), anchor, preferre...  22.6 us
    dot_general x1, matrix products, shards(): jnp.einsum('sb,bvi->svi', selector, every_mean, precision=highest)  17.2 us
  transfers between devices with their start and end apart: 1, of which 1 were waited for; matrix products, arithmetic and copies ran while one was open for 1% of the time, Pallas kernels for 0%

profile of v1, /device:TPU:0, one launch (start us, length us, event | category | flops | bytes accessed | tf_op | source)
XLA Modules:
  0.0 528.5 jit_solution(768491632789741028)
XLA Ops:
  8.7 22.6 %fusion.12 = f32[16,896,128]{2,0,1:T(8,128)S(1)} fusion(bf16[16,896,128]{2,1,0:T(8,128)(2,1)} %param.14, bf16[16,896,128]{2,1,0:T(8,128)(2,1)} %param.15, bf16[8,896,128]{2,1,0:T(8,128)(2,1)S(1)} %copy-done, s32[16]{0:T(128)S(1)} %dynamic-slice_bitcast_fusion), kind=kOutput, calls=%fused_computation.15 | convolution fusion | flops 36700544 | bytes 16515136 | tf_op jit(solution)/shard_map/sb,bvi->svi/dot_general | solution.py:43
  31.3 5.2 copy.27
  40.4 322.9 %while.13 = (s32[]{:T(128)}, f32[16,896,128]{2,1,0:T(8,128)}, f32[16,350]{1,0:T(8,128)S(1)}, bf16[16,128,128]{2,1,0:T(8,128)(2,1)S(1)}, f32[16,896,128]{2,1,0:T(...) while((s32[]{:T(128)}, f32[16,896,128]{2,1,0:T(8,128)}, ...), condition=%wide.region_3.0_spmd.clone, body=%wide.region_0.0_spmd.clone.sunk | while | flops 607978752 | bytes 75437192 | solution.py:66
  47.0 5.9 %multiply_subtract_fusion.2 = f32[16,896,128]{2,1,0:T(8,128)} fusion(f32[16,896,128]{2,1,0:T(8,128)S(1)} %copy.53, f32[16,896,128]{2,1,0:T(8,128)S(1)} %copy-done.1, f32[896,128]{1,0:T(8,128)S(1)} %get-tuple-element.187, f32[16,896]{1,0:T(8,128)S(1)} %fusion.47, bf16[16,128,128]{2,1,0:T(8,128)(2,1)S(1)} %get-tuple-element.185), kind=kOutput, calls=%fused_computation.2.clone.1 | convolution fusion | flops 482607104 | bytes 23060480 | tf_op jit(solution)/shard_map/while/body/eval_jaxpr/svi,sij->svj/dot_general | solution.py:55
  53.8 15.1 %all-gather.3 = f32[64,350]{1,0:T(8,128)S(1)} all-gather(f32[16,350]{1,0:T(8,128)S(1)} %fusion.48), channel_id=2, replica_groups=mesh['scen'=8,'veh'=4] {'veh'}, dimensions={0}, use_global_device_ids=true | all-gather | bytes 112000 | tf_op jit(solution)/shard_map/while/body/eval_jaxpr/all_gather | solution.py:15
  75.5 5.9 %multiply_subtract_fusion.2 = f32[16,896,128]{2,1,0:T(8,128)} fusion(f32[16,896,128]{2,1,0:T(8,128)S(1)} %copy.53, f32[16,896,128]{2,1,0:T(8,128)S(1)} %copy-done.1, f32[896,128]{1,0:T(8,128)S(1)} %get-tuple-element.187, f32[16,896]{1,0:T(8,128)S(1)} %fusion.47, bf16[16,128,128]{2,1,0:T(8,128)(2,1)S(1)} %get-tuple-element.185), kind=kOutput, calls=%fused_computation.2.clone.1 | convolution fusion | flops 482607104 | bytes 23060480 | tf_op jit(solution)/shard_map/while/body/eval_jaxpr/svi,sij->svj/dot_general | solution.py:55
  82.3 13.5 %all-gather.3 = f32[64,350]{1,0:T(8,128)S(1)} all-gather(f32[16,350]{1,0:T(8,128)S(1)} %fusion.48), channel_id=2, replica_groups=mesh['scen'=8,'veh'=4] {'veh'}, dimensions={0}, use_global_device_ids=true | all-gather | bytes 112000 | tf_op jit(solution)/shard_map/while/body/eval_jaxpr/all_gather | solution.py:15
  102.4 5.9 %multiply_subtract_fusion.2 = f32[16,896,128]{2,1,0:T(8,128)} fusion(f32[16,896,128]{2,1,0:T(8,128)S(1)} %copy.53, f32[16,896,128]{2,1,0:T(8,128)S(1)} %copy-done.1, f32[896,128]{1,0:T(8,128)S(1)} %get-tuple-element.187, f32[16,896]{1,0:T(8,128)S(1)} %fusion.47, bf16[16,128,128]{2,1,0:T(8,128)(2,1)S(1)} %get-tuple-element.185), kind=kOutput, calls=%fused_computation.2.clone.1 | convolution fusion | flops 482607104 | bytes 23060480 | tf_op jit(solution)/shard_map/while/body/eval_jaxpr/svi,sij->svj/dot_general | solution.py:55
  109.2 13.2 %all-gather.3 = f32[64,350]{1,0:T(8,128)S(1)} all-gather(f32[16,350]{1,0:T(8,128)S(1)} %fusion.48), channel_id=2, replica_groups=mesh['scen'=8,'veh'=4] {'veh'}, dimensions={0}, use_global_device_ids=true | all-gather | bytes 112000 | tf_op jit(solution)/shard_map/while/body/eval_jaxpr/all_gather | solution.py:15
  129.0 5.9 %multiply_subtract_fusion.2 = f32[16,896,128]{2,1,0:T(8,128)} fusion(f32[16,896,128]{2,1,0:T(8,128)S(1)} %copy.53, f32[16,896,128]{2,1,0:T(8,128)S(1)} %copy-done.1, f32[896,128]{1,0:T(8,128)S(1)} %get-tuple-element.187, f32[16,896]{1,0:T(8,128)S(1)} %fusion.47, bf16[16,128,128]{2,1,0:T(8,128)(2,1)S(1)} %get-tuple-element.185), kind=kOutput, calls=%fused_computation.2.clone.1 | convolution fusion | flops 482607104 | bytes 23060480 | tf_op jit(solution)/shard_map/while/body/eval_jaxpr/svi,sij->svj/dot_general | solution.py:55
  135.9 13.3 %all-gather.3 = f32[64,350]{1,0:T(8,128)S(1)} all-gather(f32[16,350]{1,0:T(8,128)S(1)} %fusion.48), channel_id=2, replica_groups=mesh['scen'=8,'veh'=4] {'veh'}, dimensions={0}, use_global_device_ids=true | all-gather | bytes 112000 | tf_op jit(solution)/shard_map/while/body/eval_jaxpr/all_gather | solution.py:15
  155.8 5.9 %multiply_subtract_fusion.2 = f32[16,896,128]{2,1,0:T(8,128)} fusion(f32[16,896,128]{2,1,0:T(8,128)S(1)} %copy.53, f32[16,896,128]{2,1,0:T(8,128)S(1)} %copy-done.1, f32[896,128]{1,0:T(8,128)S(1)} %get-tuple-element.187, f32[16,896]{1,0:T(8,128)S(1)} %fusion.47, bf16[16,128,128]{2,1,0:T(8,128)(2,1)S(1)} %get-tuple-element.185), kind=kOutput, calls=%fused_computation.2.clone.1 | convolution fusion | flops 482607104 | bytes 23060480 | tf_op jit(solution)/shard_map/while/body/eval_jaxpr/svi,sij->svj/dot_general | solution.py:55
  162.6 13.3 %all-gather.3 = f32[64,350]{1,0:T(8,128)S(1)} all-gather(f32[16,350]{1,0:T(8,128)S(1)} %fusion.48), channel_id=2, replica_groups=mesh['scen'=8,'veh'=4] {'veh'}, dimensions={0}, use_global_device_ids=true | all-gather | bytes 112000 | tf_op jit(solution)/shard_map/while/body/eval_jaxpr/all_gather | solution.py:15
  182.6 5.9 %multiply_subtract_fusion.2 = f32[16,896,128]{2,1,0:T(8,128)} fusion(f32[16,896,128]{2,1,0:T(8,128)S(1)} %copy.53, f32[16,896,128]{2,1,0:T(8,128)S(1)} %copy-done.1, f32[896,128]{1,0:T(8,128)S(1)} %get-tuple-element.187, f32[16,896]{1,0:T(8,128)S(1)} %fusion.47, bf16[16,128,128]{2,1,0:T(8,128)(2,1)S(1)} %get-tuple-element.185), kind=kOutput, calls=%fused_computation.2.clone.1 | convolution fusion | flops 482607104 | bytes 23060480 | tf_op jit(solution)/shard_map/while/body/eval_jaxpr/svi,sij->svj/dot_general | solution.py:55
  189.4 13.3 %all-gather.3 = f32[64,350]{1,0:T(8,128)S(1)} all-gather(f32[16,350]{1,0:T(8,128)S(1)} %fusion.48), channel_id=2, replica_groups=mesh['scen'=8,'veh'=4] {'veh'}, dimensions={0}, use_global_device_ids=true | all-gather | bytes 112000 | tf_op jit(solution)/shard_map/while/body/eval_jaxpr/all_gather | solution.py:15
  209.3 5.9 %multiply_subtract_fusion.2 = f32[16,896,128]{2,1,0:T(8,128)} fusion(f32[16,896,128]{2,1,0:T(8,128)S(1)} %copy.53, f32[16,896,128]{2,1,0:T(8,128)S(1)} %copy-done.1, f32[896,128]{1,0:T(8,128)S(1)} %get-tuple-element.187, f32[16,896]{1,0:T(8,128)S(1)} %fusion.47, bf16[16,128,128]{2,1,0:T(8,128)(2,1)S(1)} %get-tuple-element.185), kind=kOutput, calls=%fused_computation.2.clone.1 | convolution fusion | flops 482607104 | bytes 23060480 | tf_op jit(solution)/shard_map/while/body/eval_jaxpr/svi,sij->svj/dot_general | solution.py:55
  216.1 13.3 %all-gather.3 = f32[64,350]{1,0:T(8,128)S(1)} all-gather(f32[16,350]{1,0:T(8,128)S(1)} %fusion.48), channel_id=2, replica_groups=mesh['scen'=8,'veh'=4] {'veh'}, dimensions={0}, use_global_device_ids=true | all-gather | bytes 112000 | tf_op jit(solution)/shard_map/while/body/eval_jaxpr/all_gather | solution.py:15
  236.0 5.9 %multiply_subtract_fusion.2 = f32[16,896,128]{2,1,0:T(8,128)} fusion(f32[16,896,128]{2,1,0:T(8,128)S(1)} %copy.53, f32[16,896,128]{2,1,0:T(8,128)S(1)} %copy-done.1, f32[896,128]{1,0:T(8,128)S(1)} %get-tuple-element.187, f32[16,896]{1,0:T(8,128)S(1)} %fusion.47, bf16[16,128,128]{2,1,0:T(8,128)(2,1)S(1)} %get-tuple-element.185), kind=kOutput, calls=%fused_computation.2.clone.1 | convolution fusion | flops 482607104 | bytes 23060480 | tf_op jit(solution)/shard_map/while/body/eval_jaxpr/svi,sij->svj/dot_general | solution.py:55
  242.8 13.3 %all-gather.3 = f32[64,350]{1,0:T(8,128)S(1)} all-gather(f32[16,350]{1,0:T(8,128)S(1)} %fusion.48), channel_id=2, replica_groups=mesh['scen'=8,'veh'=4] {'veh'}, dimensions={0}, use_global_device_ids=true | all-gather | bytes 112000 | tf_op jit(solution)/shard_map/while/body/eval_jaxpr/all_gather | solution.py:15
  262.8 5.9 %multiply_subtract_fusion.2 = f32[16,896,128]{2,1,0:T(8,128)} fusion(f32[16,896,128]{2,1,0:T(8,128)S(1)} %copy.53, f32[16,896,128]{2,1,0:T(8,128)S(1)} %copy-done.1, f32[896,128]{1,0:T(8,128)S(1)} %get-tuple-element.187, f32[16,896]{1,0:T(8,128)S(1)} %fusion.47, bf16[16,128,128]{2,1,0:T(8,128)(2,1)S(1)} %get-tuple-element.185), kind=kOutput, calls=%fused_computation.2.clone.1 | convolution fusion | flops 482607104 | bytes 23060480 | tf_op jit(solution)/shard_map/while/body/eval_jaxpr/svi,sij->svj/dot_general | solution.py:55
  269.6 13.3 %all-gather.3 = f32[64,350]{1,0:T(8,128)S(1)} all-gather(f32[16,350]{1,0:T(8,128)S(1)} %fusion.48), channel_id=2, replica_groups=mesh['scen'=8,'veh'=4] {'veh'}, dimensions={0}, use_global_device_ids=true | all-gather | bytes 112000 | tf_op jit(solution)/shard_map/while/body/eval_jaxpr/all_gather | solution.py:15
  289.6 5.9 %multiply_subtract_fusion.2 = f32[16,896,128]{2,1,0:T(8,128)} fusion(f32[16,896,128]{2,1,0:T(8,128)S(1)} %copy.53, f32[16,896,128]{2,1,0:T(8,128)S(1)} %copy-done.1, f32[896,128]{1,0:T(8,128)S(1)} %get-tuple-element.187, f32[16,896]{1,0:T(8,128)S(1)} %fusion.47, bf16[16,128,128]{2,1,0:T(8,128)(2,1)S(1)} %get-tuple-element.185), kind=kOutput, calls=%fused_computation.2.clone.1 | convolution fusion | flops 482607104 | bytes 23060480 | tf_op jit(solution)/shard_map/while/body/eval_jaxpr/svi,sij->svj/dot_general | solution.py:55
  296.4 13.2 %all-gather.3 = f32[64,350]{1,0:T(8,128)S(1)} all-gather(f32[16,350]{1,0:T(8,128)S(1)} %fusion.48), channel_id=2, replica_groups=mesh['scen'=8,'veh'=4] {'veh'}, dimensions={0}, use_global_device_ids=true | all-gather | bytes 112000 | tf_op jit(solution)/shard_map/while/body/eval_jaxpr/all_gather | solution.py:15
  316.2 5.9 %multiply_subtract_fusion.2 = f32[16,896,128]{2,1,0:T(8,128)} fusion(f32[16,896,128]{2,1,0:T(8,128)S(1)} %copy.53, f32[16,896,128]{2,1,0:T(8,128)S(1)} %copy-done.1, f32[896,128]{1,0:T(8,128)S(1)} %get-tuple-element.187, f32[16,896]{1,0:T(8,128)S(1)} %fusion.47, bf16[16,128,128]{2,1,0:T(8,128)(2,1)S(1)} %get-tuple-element.185), kind=kOutput, calls=%fused_computation.2.clone.1 | convolution fusion | flops 482607104 | bytes 23060480 | tf_op jit(solution)/shard_map/while/body/eval_jaxpr/svi,sij->svj/dot_general | solution.py:55
  323.1 13.4 %all-gather.3 = f32[64,350]{1,0:T(8,128)S(1)} all-gather(f32[16,350]{1,0:T(8,128)S(1)} %fusion.48), channel_id=2, replica_groups=mesh['scen'=8,'veh'=4] {'veh'}, dimensions={0}, use_global_device_ids=true | all-gather | bytes 112000 | tf_op jit(solution)/shard_map/while/body/eval_jaxpr/all_gather | solution.py:15
  343.1 5.9 %multiply_subtract_fusion.2 = f32[16,896,128]{2,1,0:T(8,128)} fusion(f32[16,896,128]{2,1,0:T(8,128)S(1)} %copy.53, f32[16,896,128]{2,1,0:T(8,128)S(1)} %copy-done.1, f32[896,128]{1,0:T(8,128)S(1)} %get-tuple-element.187, f32[16,896]{1,0:T(8,128)S(1)} %fusion.47, bf16[16,128,128]{2,1,0:T(8,128)(2,1)S(1)} %get-tuple-element.185), kind=kOutput, calls=%fused_computation.2.clone.1 | convolution fusion | flops 482607104 | bytes 23060480 | tf_op jit(solution)/shard_map/while/body/eval_jaxpr/svi,sij->svj/dot_general | solution.py:55
  349.9 13.3 %all-gather.3 = f32[64,350]{1,0:T(8,128)S(1)} all-gather(f32[16,350]{1,0:T(8,128)S(1)} %fusion.48), channel_id=2, replica_groups=mesh['scen'=8,'veh'=4] {'veh'}, dimensions={0}, use_global_device_ids=true | all-gather | bytes 112000 | tf_op jit(solution)/shard_map/while/body/eval_jaxpr/all_gather | solution.py:15
  363.4 14.0 %fusion.14 = f32[8,896,128]{2,0,1:T(8,128)} fusion(f32[16,896,128]{2,1,0:T(8,128)} %get-tuple-element.48, f32[16]{0:T(128)S(1)} %dynamic-slice_convert_fusion.1, s32[16]{0:T(128)S(1)} %dynamic-slice_bitcast_fusion), kind=kOutput, calls=%fused_computation.18 | convolution fusion | flops 176161024 | bytes 11010176 | tf_op jit(solution)/shard_map/sb,svi->bvi/dot_general | solution.py:77
  377.4 5.6 %convert_element_type.49 = bf16[16,896,128]{2,1,0:T(8,128)(2,1)} convert(f32[16,896,128]{2,1,0:T(8,128)} %get-tuple-element.48) | non-fusion elementwise | flops 1835008 | bytes 11010048 | tf_op jit(solution)/shard_map/convert_element_type | solution.py:88
  384.4 69.0 %all-reduce.2.cloned.1.call-done = f32[8,896,128]{2,0,1:T(8,128)} async-done(((f32[8,896,128]{2,0,1:T(8,128)}), f32[8,896,128]{2,0,1:T(8,128)}) %all-reduce.2.cloned.1.call-update) | async-done | bytes 3670032 | tf_op jit(solution)/shard_map/psum | solution.py:78
  456.5 17.2 %multiply_reduce_fusion.1 = (f32[16]{0:T(128)S(1)}, bf16[16,896,128]{2,0,1:T(8,128)(2,1)S(1)}) fusion(bf16[16,896,128]{2,1,0:T(8,128)(2,1)S(1)} %copy-done.3, f32[8,896,128]{2,0,1:T(8,128)S(1)} %broadcast_divide_fusion, s32[16]{0:T(128)S(1)} %dynamic-slice_bitcast_fusion, f32[16,896,128]{2,1,0:T(8,128)} %get-tuple-element.48), kind=kOutput, calls=%fused_computation.17 | convolution fusion | flops 187170928 | bytes 18350208 | tf_op jit(solution)/shard_map/sb,bvi->svi/dot_general | solution.py:81
  477.2 39.5 %psum.15 = f32[]{:T(128)} all-reduce(f32[]{:T(128)} %multiply_reduce_fusion.2), channel_id=1, replica_groups=mesh['scen'=8,'veh'=4] {'scen','veh'}, use_global_device_ids=true, to_apply=%region_8.0 | all-reduce | flops 1 | bytes 8 | tf_op jit(solution)/shard_map/psum | solution.py:85
  (134 shorter events, 106.1 us)
Async XLA Ops:
  7.2 1.5 copy-start
  7.2 446.2 %all-reduce.2.cloned.1.call-start = ((), (), s32[]{:S(2)}) async-start(), calls=%async_computation | async-start | bytes 7340032 | tf_op jit(solution)/shard_map/psum | solution.py:78
  31.3 5.2 copy-start.5
  36.5 3.8 copy-start.9
  36.5 3.8 copy-start.4
  36.5 3.9 copy-start.7
  36.5 3.9 copy-start.8
  36.5 3.9 copy-start.11
  40.4 322.9 %copy-start.10 = (s32[128]{0:T(128)S(1)}, s32[128]{0:T(128)}, u32[]{:S(2)}) copy-start(s32[128]{0:T(128)} %param.23) | copy-start | bytes 1540
  43.5 3.5 copy-start.1
  72.0 3.5 copy-start.1
  98.9 3.5 copy-start.1
  125.6 3.5 copy-start.1
  152.3 3.5 copy-start.1
  179.1 3.5 copy-start.1
  205.8 3.5 copy-start.1
  232.5 3.5 copy-start.1
  259.3 3.5 copy-start.1
  286.1 3.5 copy-start.1
  312.8 3.5 copy-start.1
  339.6 3.5 copy-start.1
  363.3 14.1 %copy-start.6 = (f32[16,350]{1,0:T(8,128)}, f32[16,350]{1,0:T(8,128)S(1)}, u32[]{:S(2)}) copy-start(f32[16,350]{1,0:T(8,128)S(1)} %get-tuple-element.93) | copy-start | bytes 67204
  377.3 6.9 %copy-start.12 = (s32[128,1]{0,1:T(1,128)S(1)}, s32[128,1]{0,1:T(1,128)}, u32[]{:S(2)}) copy-start(s32[128,1]{0,1:T(1,128)} %param.22) | copy-start | bytes 1540
  453.4 3.1 copy-start.3
  456.5 17.2 %copy-start.2 = (f32[8,896,128]{2,0,1:T(8,128)}, f32[8,896,128]{2,0,1:T(8,128)S(1)}, u32[]{:S(2)}) copy-start(f32[8,896,128]{2,0,1:T(8,128)S(1)} %broadcast_divide_fusion) | copy-start | bytes 11010052
Sparse Core Ops, SparseCore 0:
  377.5 75.8 all-reduce.1
